TPU v7x, 32 devices: a whole 2x2x4 slice. The times are simulated.
32 devices in a mesh: dp: 16 (over z, x, core), tensor: 2 (over y).
Axes of the slice: x: 2, y: 2, z: 4, core: 2. Of those that a mesh axis runs over, the one named last changes fastest.
Arguments:
- x_input: bfloat16 [16, 768, 1536], P('dp', 'tensor'), may hold values from -6 to 6
- cond_tokens: bfloat16 [16, 130, 1536], P('dp'), may hold values from -6 to 6
- teacher: bfloat16 [16, 768, 1536], P('dp', 'tensor'), may hold values from -6 to 6
- valid_mask: int32 [16, 768], P('dp', 'tensor'), may hold values from 0 to 1, as said below
- norm_gains: bfloat16 [3, 1536], P(None, 'dp'), may hold values from 0.099609375 to 1.8984375
- w_query: bfloat16 [1536, 1536], P('dp', 'tensor'), may hold values from -0.15625 to 0.15625
- w_key: bfloat16 [1536, 1536], P('dp', 'tensor'), may hold values from -0.15625 to 0.15625
- w_value: bfloat16 [1536, 1536], P('dp', 'tensor'), may hold values from -0.15625 to 0.15625
- w_out: bfloat16 [1536, 1536], P('tensor', 'dp'), may hold values from -3 to 3
- c_query: bfloat16 [1536, 1536], P('dp', 'tensor'), may hold values from -0.15625 to 0.15625
- c_key: bfloat16 [1536, 1536], P('dp', 'tensor'), may hold values from -0.15625 to 0.15625
- c_value: bfloat16 [1536, 1536], P('dp', 'tensor'), may hold values from -0.15625 to 0.15625
- c_out: bfloat16 [1536, 1536], P('tensor', 'dp'), may hold values from -1.25 to 1.25
- w_gate: bfloat16 [1536, 6144], P('dp', 'tensor'), may hold values from -0.15625 to 0.15625
- w_up: bfloat16 [1536, 6144], P('dp', 'tensor'), may hold values from -0.15625 to 0.15625
- w_down: bfloat16 [6144, 1536], P('tensor', 'dp'), may hold values from -0.078125 to 0.078125
Outputs:
- output: bfloat16 [16, 768, 1536], P('dp', 'tensor')
- mean_loss: float32 [], replicated
- grad_input: float32 [16, 768, 1536], P('dp', 'tensor')
- grad_cond: float32 [16, 130, 1536], P('dp')
- grad_w_query: float32 [1536, 1536], P('dp', 'tensor')
- grad_w_key: float32 [1536, 1536], P('dp', 'tensor')
- grad_w_value: float32 [1536, 1536], P('dp', 'tensor')
- grad_w_out: float32 [1536, 1536], P('tensor', 'dp')
- grad_c_query: float32 [1536, 1536], P('dp', 'tensor')
- grad_c_key: float32 [1536, 1536], P('dp', 'tensor')
- grad_c_value: float32 [1536, 1536], P('dp', 'tensor')
- grad_c_out: float32 [1536, 1536], P('tensor', 'dp')
- grad_w_gate: float32 [1536, 6144], P('dp', 'tensor')
- grad_w_up: float32 [1536, 6144], P('dp', 'tensor')
- grad_w_down: float32 [6144, 1536], P('tensor', 'dp')
- grad_norm_gains: float32 [3, 1536], P(None, 'dp')
Inputs may be any that keep to these rules, and one draw needn't show every extreme that they name: `valid_mask`: the valid tokens of each latent form a prefix of it, and every latent has a valid token.
All inputs are finite; a program needn't handle non-finite values.
Results may differ from a plain program's by a relative error of at most 0.017.
Values may be sent and summed in bfloat16 or wider, within the bound.
No kernel may reach another device: no remote copies, remote signals or barrier semaphores. Data moves between devices by JAX's collectives and lax.ppermute only.
A program may use at most 256 MiB of HBM per device.

v0:
```python
import math
import jax
import jax.numpy as jnp
from jax import lax
from jax.sharding import PartitionSpec as P

HEAD_DIM = 64
EPSILON = 1e-05


def matmul(left_side, right_side):
    return jnp.dot(left_side, right_side, preferred_element_type=jnp.float32)


def contract_rows(left_side, right_side):
    return lax.dot_general(
        left_side, right_side, (((0,), (0,)), ((), ())), preferred_element_type=jnp.float32
    )


def times_transposed(left_side, right_side):
    return lax.dot_general(
        left_side, right_side, (((1,), (1,)), ((), ())), preferred_element_type=jnp.float32
    )


def norm_stats(values):
    row_mean = jnp.mean(values, axis=-1, keepdims=True)
    centred = values - row_mean
    row_var = jnp.mean(centred * centred, axis=-1, keepdims=True)
    inverse = lax.rsqrt(row_var + EPSILON)
    return (centred * inverse, inverse)


def norm_back(grad_normed, normed, inverse, gain_row):
    scaled = grad_normed * gain_row
    mean_scaled = jnp.mean(scaled, axis=-1, keepdims=True)
    mean_product = jnp.mean(scaled * normed, axis=-1, keepdims=True)
    grad_values = inverse * (scaled - mean_scaled - normed * mean_product)
    return (grad_values, jnp.sum(grad_normed * normed, axis=0))


def rotary_tables(length):
    half_dim = HEAD_DIM // 2
    freqs = jnp.exp(jnp.arange(half_dim, dtype=jnp.float32) * (-math.log(10000.0) / half_dim))
    angles = jnp.arange(length, dtype=jnp.float32)[:, None] * freqs[None, :]
    return (jnp.cos(angles)[:, None, :], jnp.sin(angles)[:, None, :])


def rotate(values, rot_cos, rot_sin):
    half_dim = HEAD_DIM // 2
    lower = values[..., :half_dim]
    upper = values[..., half_dim:]
    return jnp.concatenate(
        [lower * rot_cos - upper * rot_sin, upper * rot_cos + lower * rot_sin], axis=-1
    )


def rotate_back(values, rot_cos, rot_sin):
    half_dim = HEAD_DIM // 2
    lower = values[..., :half_dim]
    upper = values[..., half_dim:]
    return jnp.concatenate(
        [lower * rot_cos + upper * rot_sin, upper * rot_cos - lower * rot_sin], axis=-1
    )


def attend_forward(queries, keys_in, values_in):
    scale_factor = HEAD_DIM ** (-0.5)
    scores = (
        jnp.einsum("qhd,khd->hqk", queries, keys_in, preferred_element_type=jnp.float32)
        * scale_factor
    )
    row_max = jnp.max(scores, axis=-1, keepdims=True)
    shifted = jnp.exp(scores - row_max)
    row_total = jnp.sum(shifted, axis=-1, keepdims=True)
    soft_probs = (shifted / row_total).astype(jnp.bfloat16)
    mixed = jnp.einsum("hqk,khd->qhd", soft_probs, values_in, preferred_element_type=jnp.float32)
    return (mixed, row_max + jnp.log(row_total))


def attend_back(queries, keys_in, values_in, log_total, grad_mixed):
    scale_factor = HEAD_DIM ** (-0.5)
    scores = (
        jnp.einsum("qhd,khd->hqk", queries, keys_in, preferred_element_type=jnp.float32)
        * scale_factor
    )
    soft_probs = jnp.exp(scores - log_total)
    grad_values = jnp.einsum(
        "hqk,qhd->khd",
        soft_probs.astype(jnp.bfloat16),
        grad_mixed,
        preferred_element_type=jnp.float32,
    )
    grad_probs = jnp.einsum(
        "qhd,khd->hqk", grad_mixed, values_in, preferred_element_type=jnp.float32
    )
    weighted = jnp.sum(soft_probs * grad_probs, axis=-1, keepdims=True)
    grad_scores = (soft_probs * (grad_probs - weighted)).astype(jnp.bfloat16)
    grad_queries = (
        jnp.einsum("hqk,khd->qhd", grad_scores, keys_in, preferred_element_type=jnp.float32)
        * scale_factor
    )
    grad_keys = (
        jnp.einsum("hqk,qhd->khd", grad_scores, queries, preferred_element_type=jnp.float32)
        * scale_factor
    )
    return (grad_queries, grad_keys, grad_values)


def body(
    x_input,
    cond_tokens,
    teacher,
    valid_mask,
    norm_gains,
    w_query,
    w_key,
    w_value,
    w_out,
    c_query,
    c_key,
    c_value,
    c_out,
    w_gate,
    w_up,
    w_down,
):
    bf_type = jnp.bfloat16

    def fetch_attention():
        return (
            lax.all_gather(w_query, "dp", axis=0, tiled=True),
            lax.all_gather(w_key, "dp", axis=0, tiled=True),
            lax.all_gather(w_value, "dp", axis=0, tiled=True),
            lax.all_gather(w_out, "dp", axis=1, tiled=True),
            lax.all_gather(c_query, "dp", axis=0, tiled=True),
            lax.all_gather(c_key, "dp", axis=0, tiled=True),
            lax.all_gather(c_value, "dp", axis=0, tiled=True),
            lax.all_gather(c_out, "dp", axis=1, tiled=True),
            lax.all_gather(norm_gains, "dp", axis=1, tiled=True),
        )

    def fetch_mlp():
        return (
            lax.all_gather(w_gate, "dp", axis=0, tiled=True),
            lax.all_gather(w_up, "dp", axis=0, tiled=True),
            lax.all_gather(w_down, "dp", axis=1, tiled=True),
        )

    def gather_rows(values):
        return lax.all_gather(values, "tensor", axis=0, tiled=True)

    def scatter_rows(values):
        return lax.psum_scatter(values, "tensor", scatter_dimension=0, tiled=True)

    def gather_grads(values):
        return lax.all_gather(values, "tensor", axis=0, tiled=True)

    def scatter_grads(values):
        return lax.psum_scatter(values, "tensor", scatter_dimension=0, tiled=True)

    local_rows = x_input[0].astype(jnp.float32)
    cond_rows = cond_tokens[0]
    mask_float = valid_mask[0].astype(jnp.float32)
    width = local_rows.shape[1]
    token_total = float(lax.axis_size("dp") * lax.axis_size("tensor") * local_rows.shape[0])
    weight_q, weight_k, weight_v, weight_o, cross_q, cross_k, cross_v, cross_o, gains_bf = (
        fetch_attention()
    )
    gains = gains_bf.astype(jnp.float32)
    normed_one, inverse_one = norm_stats(local_rows)
    input_one = gather_rows((normed_one * gains[0]).astype(bf_type))
    length = input_one.shape[0]
    ctx_len = cond_rows.shape[0]
    rot_cos, rot_sin = rotary_tables(length)
    query_rot = rotate(
        matmul(input_one, weight_q).reshape(length, -1, HEAD_DIM), rot_cos, rot_sin
    ).astype(bf_type)
    key_rot = rotate(
        matmul(input_one, weight_k).reshape(length, -1, HEAD_DIM), rot_cos, rot_sin
    ).astype(bf_type)
    value_self = matmul(input_one, weight_v).astype(bf_type).reshape(length, -1, HEAD_DIM)
    mixed_self, log_self = attend_forward(query_rot, key_rot, value_self)
    mixed_self = mixed_self.reshape(length, -1).astype(bf_type)
    hidden_one = local_rows + scatter_rows(matmul(mixed_self, weight_o))
    normed_two, inverse_two = norm_stats(hidden_one)
    input_two = gather_rows((normed_two * gains[1]).astype(bf_type))
    query_cross = matmul(input_two, cross_q).astype(bf_type).reshape(length, -1, HEAD_DIM)
    key_cross = matmul(cond_rows, cross_k).astype(bf_type).reshape(ctx_len, -1, HEAD_DIM)
    value_cross = matmul(cond_rows, cross_v).astype(bf_type).reshape(ctx_len, -1, HEAD_DIM)
    mixed_cross, log_cross = attend_forward(query_cross, key_cross, value_cross)
    mixed_cross = mixed_cross.reshape(length, -1).astype(bf_type)
    hidden_two = hidden_one + scatter_rows(matmul(mixed_cross, cross_o))
    weight_gate, weight_up, weight_down = fetch_mlp()
    normed_three, inverse_three = norm_stats(hidden_two)
    input_three = gather_rows((normed_three * gains[2]).astype(bf_type))
    gate_pre = matmul(input_three, weight_gate)
    up_pre = matmul(input_three, weight_up)
    gate_sigmoid = jax.nn.sigmoid(gate_pre)
    gate_silu = gate_pre * gate_sigmoid
    hidden_ff = (gate_silu * up_pre).astype(bf_type)
    block_out = hidden_two + scatter_rows(matmul(hidden_ff, weight_down))
    error_diff = block_out - teacher[0].astype(jnp.float32)
    local_error = jnp.sum(mask_float[:, None] * error_diff * error_diff)
    valid_count, error_total = lax.psum((jnp.sum(mask_float), local_error), ("dp", "tensor"))
    mean_loss = error_total / (width * valid_count)
    grad_out = 2.0 * token_total / valid_count * mask_float[:, None] * error_diff
    weight_gate, weight_up, weight_down = fetch_mlp()
    branch_three = gather_grads(grad_out.astype(bf_type))
    grad_hidden = times_transposed(branch_three, weight_down)
    grad_down = contract_rows(hidden_ff, branch_three)
    grad_gate = (
        grad_hidden * up_pre * gate_sigmoid * (1.0 + gate_pre * (1.0 - gate_sigmoid))
    ).astype(bf_type)
    grad_upper = (grad_hidden * gate_silu).astype(bf_type)
    grad_gate_w = contract_rows(input_three, grad_gate)
    grad_up_w = contract_rows(input_three, grad_upper)
    grad_normed_three = scatter_grads(
        times_transposed(grad_gate, weight_gate) + times_transposed(grad_upper, weight_up)
    )
    grad_gate_s, grad_up_s, grad_down_s = (
        lax.psum_scatter(grad_gate_w, "dp", scatter_dimension=0, tiled=True),
        lax.psum_scatter(grad_up_w, "dp", scatter_dimension=0, tiled=True),
        lax.psum_scatter(grad_down, "dp", scatter_dimension=1, tiled=True),
    )
    back_three, gain_three = norm_back(grad_normed_three, normed_three, inverse_three, gains[2])
    grad_two = grad_out + back_three
    weight_q, weight_k, weight_v, weight_o, cross_q, cross_k, cross_v, cross_o, spare_gains = (
        fetch_attention()
    )
    branch_two = gather_grads(grad_two.astype(bf_type))
    grad_cross_o = contract_rows(mixed_cross, branch_two)
    grad_mixed_cross = (
        times_transposed(branch_two, cross_o).astype(bf_type).reshape(length, -1, HEAD_DIM)
    )
    grad_qc, grad_kc, grad_vc = attend_back(
        query_cross, key_cross, value_cross, log_cross, grad_mixed_cross
    )
    grad_qc = grad_qc.reshape(length, -1).astype(bf_type)
    grad_kc = grad_kc.reshape(ctx_len, -1).astype(bf_type)
    grad_vc = grad_vc.reshape(ctx_len, -1).astype(bf_type)
    grad_cross_q = contract_rows(input_two, grad_qc)
    grad_cross_k = contract_rows(cond_rows, grad_kc)
    grad_cross_v = contract_rows(cond_rows, grad_vc)
    cond_part = times_transposed(grad_kc, cross_k) + times_transposed(grad_vc, cross_v)
    grad_normed_two = scatter_grads(times_transposed(grad_qc, cross_q))
    back_two, gain_two = norm_back(grad_normed_two, normed_two, inverse_two, gains[1])
    grad_one = grad_two + back_two
    branch_one = gather_grads(grad_one.astype(bf_type))
    grad_self_o = contract_rows(mixed_self, branch_one)
    grad_mixed_self = (
        times_transposed(branch_one, weight_o).astype(bf_type).reshape(length, -1, HEAD_DIM)
    )
    grad_qs, grad_ks, grad_vs = attend_back(
        query_rot, key_rot, value_self, log_self, grad_mixed_self
    )
    grad_qs = rotate_back(grad_qs, rot_cos, rot_sin).reshape(length, -1).astype(bf_type)
    grad_ks = rotate_back(grad_ks, rot_cos, rot_sin).reshape(length, -1).astype(bf_type)
    grad_vs = grad_vs.reshape(length, -1).astype(bf_type)
    grad_self_q = contract_rows(input_one, grad_qs)
    grad_self_k = contract_rows(input_one, grad_ks)
    grad_self_v = contract_rows(input_one, grad_vs)
    grad_normed_one = scatter_grads(
        times_transposed(grad_qs, weight_q)
        + times_transposed(grad_ks, weight_k)
        + times_transposed(grad_vs, weight_v)
    )
    back_one, gain_one = norm_back(grad_normed_one, normed_one, inverse_one, gains[0])
    grad_rows = grad_one + back_one
    gain_part = jnp.stack([gain_one, gain_two, gain_three])
    cond_sum, gain_sum = (
        lax.psum(cond_part.astype(jnp.bfloat16), "tensor").astype(jnp.float32),
        lax.psum(gain_part.astype(jnp.bfloat16), "tensor").astype(jnp.float32),
    )
    (
        grad_q_s,
        grad_k_s,
        grad_v_s,
        grad_o_s,
        grad_cq_s,
        grad_ck_s,
        grad_cv_s,
        grad_co_s,
        grad_gain_s,
    ) = (
        lax.psum_scatter(grad_self_q, "dp", scatter_dimension=0, tiled=True),
        lax.psum_scatter(grad_self_k, "dp", scatter_dimension=0, tiled=True),
        lax.psum_scatter(grad_self_v, "dp", scatter_dimension=0, tiled=True),
        lax.psum_scatter(grad_self_o, "dp", scatter_dimension=1, tiled=True),
        lax.psum_scatter(grad_cross_q, "dp", scatter_dimension=0, tiled=True),
        lax.psum_scatter(grad_cross_k, "dp", scatter_dimension=0, tiled=True),
        lax.psum_scatter(grad_cross_v, "dp", scatter_dimension=0, tiled=True),
        lax.psum_scatter(grad_cross_o, "dp", scatter_dimension=1, tiled=True),
        lax.psum_scatter(gain_sum, "dp", scatter_dimension=1, tiled=True),
    )
    return (
        block_out.astype(bf_type)[None],
        mean_loss,
        grad_rows[None],
        cond_sum[None],
        grad_q_s,
        grad_k_s,
        grad_v_s,
        grad_o_s,
        grad_cq_s,
        grad_ck_s,
        grad_cv_s,
        grad_co_s,
        grad_gate_s,
        grad_up_s,
        grad_down_s,
        grad_gain_s,
    )


def solution(mesh):
    return jax.shard_map(
        body,
        mesh=mesh,
        in_specs=(
            P("dp", "tensor", None),
            P("dp", None, None),
            P("dp", "tensor", None),
            P("dp", "tensor"),
            P(None, "dp"),
            P("dp", "tensor"),
            P("dp", "tensor"),
            P("dp", "tensor"),
            P("tensor", "dp"),
            P("dp", "tensor"),
            P("dp", "tensor"),
            P("dp", "tensor"),
            P("tensor", "dp"),
            P("dp", "tensor"),
            P("dp", "tensor"),
            P("tensor", "dp"),
        ),
        out_specs=(
            P("dp", "tensor", None),
            P(),
            P("dp", "tensor", None),
            P("dp", None, None),
            P("dp", "tensor"),
            P("dp", "tensor"),
            P("dp", "tensor"),
            P("tensor", "dp"),
            P("dp", "tensor"),
            P("dp", "tensor"),
            P("dp", "tensor"),
            P("tensor", "dp"),
            P("dp", "tensor"),
            P("dp", "tensor"),
            P("tensor", "dp"),
            P(None, "dp"),
        ),
        check_vma=False,
    )
```

profile of v0, /device:TPU:0, one launch (start us, length us, event | category | flops | bytes accessed | tf_op | source)
XLA Modules:
  0.0 2735.1 jit_solution(5155967029090758559)
XLA Ops:
  39.1 30.3 %all-gather.19.cloned.1.call-done = bf16[768,1536]{1,0:T(8,128)(2,1)} async-done(((bf16[384,1536]{1,0:T(8,128)(2,1)}), bf16[768,1536]{1,0:T(8,128)(2,1)}) %all-gather.19.cloned.1.call-update) | async-done | bytes 2359312 | tf_op jit(solution)/shard_map/all_gather | solution.py:152
  69.5 44.6 %all-gather.25.cloned.1.call-done = bf16[1536,768]{1,0:T(8,128)(2,1)} async-done(((bf16[96,768]{1,0:T(8,128)(2,1)}), bf16[1536,768]{1,0:T(8,128)(2,1)}) %all-gather.25.cloned.1.call-update) | async-done | bytes 2359312 | tf_op jit(solution)/shard_map/all_gather | solution.py:134
  118.6 38.9 %all-gather.23.cloned.1.call-done = bf16[1536,768]{1,0:T(8,128)(2,1)} async-done(((bf16[96,768]{1,0:T(8,128)(2,1)}), bf16[1536,768]{1,0:T(8,128)(2,1)}) %all-gather.23.cloned.1.call-update) | async-done | bytes 2359312 | tf_op jit(solution)/shard_map/all_gather | solution.py:133
  252.2 56.6 %reduce-scatter.25.cloned.1.call-done = f32[384,1536]{1,0:T(8,128)} async-done(((f32[768,1536]{1,0:T(8,128)}), f32[384,1536]{1,0:T(8,128)}) %reduce-scatter.25.cloned.1.call-update) | async-done | bytes 2359312 | tf_op jit(solution)/shard_map/reduce_scatter | solution.py:155
  314.0 39.8 %all-gather.29.cloned.1.call-done = bf16[1536,768]{1,0:T(8,128)(2,1)} async-done(((bf16[96,768]{1,0:T(8,128)(2,1)}), bf16[1536,768]{1,0:T(8,128)(2,1)}) %all-gather.29.cloned.1.call-update) | async-done | bytes 2359312 | tf_op jit(solution)/shard_map/all_gather | solution.py:139
  356.9 40.6 %all-gather.35.cloned.1.call-done = bf16[1536,768]{1,0:T(8,128)(2,1)} async-done(((bf16[96,768]{1,0:T(8,128)(2,1)}), bf16[1536,768]{1,0:T(8,128)(2,1)}) %all-gather.35.cloned.1.call-update) | async-done | bytes 2359312 | tf_op jit(solution)/shard_map/all_gather | solution.py:138
  399.8 41.3 %all-gather.33.cloned.1.call-done = bf16[1536,768]{1,0:T(8,128)(2,1)} async-done(((bf16[96,768]{1,0:T(8,128)(2,1)}), bf16[1536,768]{1,0:T(8,128)(2,1)}) %all-gather.33.cloned.1.call-update) | async-done | bytes 2359312 | tf_op jit(solution)/shard_map/all_gather | solution.py:137
  441.1 36.9 %all-gather.31.cloned.1.call-done = bf16[768,1536]{1,0:T(8,128)(2,1)} async-done(((bf16[384,1536]{1,0:T(8,128)(2,1)}), bf16[768,1536]{1,0:T(8,128)(2,1)}) %all-gather.31.cloned.1.call-update) | async-done | bytes 2359312 | tf_op jit(solution)/shard_map/all_gather | solution.py:152
  488.3 34.7 %all-gather.37.cloned.1.call-done = bf16[768,1536]{0,1:T(8,128)(2,1)} async-done(((bf16[768,96]{0,1:T(8,128)(2,1)}), bf16[768,1536]{0,1:T(8,128)(2,1)}) %all-gather.37.cloned.1.call-update) | async-done | bytes 2359312 | tf_op jit(solution)/shard_map/all_gather | solution.py:140
  530.0 58.1 %reduce-scatter.27.cloned.1.call-done = f32[384,1536]{1,0:T(8,128)} async-done(((f32[768,1536]{1,0:T(8,128)}), f32[384,1536]{1,0:T(8,128)}) %reduce-scatter.27.cloned.1.call-update) | async-done | bytes 2359312 | tf_op jit(solution)/shard_map/reduce_scatter | solution.py:155
  594.5 77.3 %all-gather.41.cloned.1.call-done = bf16[1536,3072]{1,0:T(8,128)(2,1)} async-done(((bf16[96,3072]{1,0:T(8,128)(2,1)}), bf16[1536,3072]{1,0:T(8,128)(2,1)}) %all-gather.41.cloned.1.call-update) | async-done | bytes 9437200 | tf_op jit(solution)/shard_map/all_gather | solution.py:146
  671.9 36.2 %all-gather.39.cloned.1.call-done = bf16[768,1536]{1,0:T(8,128)(2,1)} async-done(((bf16[384,1536]{1,0:T(8,128)(2,1)}), bf16[768,1536]{1,0:T(8,128)(2,1)}) %all-gather.39.cloned.1.call-update) | async-done | bytes 2359312 | tf_op jit(solution)/shard_map/all_gather | solution.py:152
  722.2 69.5 %all-gather.43.cloned.1.call-done = bf16[1536,3072]{1,0:T(8,128)(2,1)} async-done(((bf16[96,3072]{1,0:T(8,128)(2,1)}), bf16[1536,3072]{1,0:T(8,128)(2,1)}) %all-gather.43.cloned.1.call-update) | async-done | bytes 9437200 | tf_op jit(solution)/shard_map/all_gather | solution.py:147
  808.0 65.4 %all-gather.45.cloned.1.call-done = bf16[3072,1536]{0,1:T(8,128)(2,1)} async-done(((bf16[3072,96]{0,1:T(8,128)(2,1)}), bf16[3072,1536]{0,1:T(8,128)(2,1)}) %all-gather.45.cloned.1.call-update) | async-done | bytes 9437200 | tf_op jit(solution)/shard_map/all_gather | solution.py:148
  887.7 39.0 %psum.29 = f32[]{:T(128)} all-reduce(f32[]{:T(128)} %get-tuple-element.93), channel_id=1, replica_groups=mesh['dp'=16,'tensor'=2] {'dp','tensor'}, use_global_device_ids=true, to_apply=%region_16.0 | all-reduce | flops 1 | bytes 8 | tf_op jit(solution)/shard_map/psum | solution.py:206
  950.2 35.6 %all-gather.47.cloned.1.call-done = bf16[768,1536]{1,0:T(8,128)(2,1)} async-done(((bf16[384,1536]{1,0:T(8,128)(2,1)}), bf16[768,1536]{1,0:T(8,128)(2,1)}) %all-gather.47.cloned.1.call-update) | async-done | bytes 2359312 | tf_op jit(solution)/shard_map/all_gather | solution.py:158
  1029.3 60.1 %reduce-scatter.31.cloned.1.call-done = f32[384,1536]{1,0:T(8,128)} async-done(((f32[768,1536]{1,0:T(8,128)}), f32[384,1536]{1,0:T(8,128)}) %reduce-scatter.31.cloned.1.call-update) | async-done | bytes 2359312 | tf_op jit(solution)/shard_map/reduce_scatter | solution.py:161
  1097.9 36.0 %all-gather.49.cloned.1.call-done = bf16[768,1536]{1,0:T(8,128)(2,1)} async-done(((bf16[384,1536]{1,0:T(8,128)(2,1)}), bf16[768,1536]{1,0:T(8,128)(2,1)}) %all-gather.49.cloned.1.call-update) | async-done | bytes 2359312 | tf_op jit(solution)/shard_map/all_gather | solution.py:158
  1151.6 60.1 %reduce-scatter.33.cloned.1.call-done = f32[384,1536]{1,0:T(8,128)} async-done(((f32[768,1536]{1,0:T(8,128)}), f32[384,1536]{1,0:T(8,128)}) %reduce-scatter.33.cloned.1.call-update) | async-done | bytes 2359312 | tf_op jit(solution)/shard_map/reduce_scatter | solution.py:161
  1217.8 35.9 %all-gather.51.cloned.1.call-done = bf16[768,1536]{1,0:T(8,128)(2,1)} async-done(((bf16[384,1536]{1,0:T(8,128)(2,1)}), bf16[768,1536]{1,0:T(8,128)(2,1)}) %all-gather.51.cloned.1.call-update) | async-done | bytes 2359312 | tf_op jit(solution)/shard_map/all_gather | solution.py:158
  1356.9 48.8 %reduce-scatter.35.cloned.1.call-done = f32[384,1536]{1,0:T(8,128)} async-done(((f32[768,1536]{1,0:T(8,128)}), f32[384,1536]{1,0:T(8,128)}) %reduce-scatter.35.cloned.1.call-update) | async-done | bytes 2359312 | tf_op jit(solution)/shard_map/reduce_scatter | solution.py:161
  1519.5 42.2 %psum.28 = f32[]{:T(128)} all-reduce(f32[]{:T(128)} %get-tuple-element.89), channel_id=1, replica_groups=mesh['dp'=16,'tensor'=2] {'dp','tensor'}, use_global_device_ids=true, to_apply=%region_14.0 | all-reduce | flops 1 | bytes 8 | tf_op jit(solution)/shard_map/psum | solution.py:206
  1575.0 78.9 %reduce-scatter.45.cloned.1.call-done = f32[96,768]{1,0:T(8,128)} async-done(((f32[1536,768]{1,0:T(8,128)}), f32[96,768]{1,0:T(8,128)}) %reduce-scatter.45.cloned.1.call-update) | async-done | bytes 294928 | tf_op jit(solution)/shard_map/reduce_scatter | solution.py:291
  1653.9 79.6 %reduce-scatter.57.cloned.1.call-done = f32[96,768]{1,0:T(8,128)} async-done(((f32[1536,768]{1,0:T(8,128)}), f32[96,768]{1,0:T(8,128)}) %reduce-scatter.57.cloned.1.call-update) | async-done | bytes 294928
  1733.5 79.1 %reduce-scatter.55.cloned.1.call-done = f32[96,768]{1,0:T(8,128)} async-done(((f32[1536,768]{1,0:T(8,128)}), f32[96,768]{1,0:T(8,128)}) %reduce-scatter.55.cloned.1.call-update) | async-done | bytes 294928
  1812.6 198.9 %reduce-scatter.53.cloned.1.call-done = f32[3072,96]{0,1:T(8,128)} async-done(((f32[3072,1536]{0,1:T(8,128)}), f32[3072,96]{0,1:T(8,128)}) %reduce-scatter.53.cloned.1.call-update) | async-done | bytes 1179664 | tf_op jit(solution)/shard_map/reduce_scatter | solution.py:225
  2011.5 199.2 %reduce-scatter.51.cloned.1.call-done = f32[96,3072]{1,0:T(8,128)} async-done(((f32[1536,3072]{1,0:T(8,128)}), f32[96,3072]{1,0:T(8,128)}) %reduce-scatter.51.cloned.1.call-update) | async-done | bytes 1179664 | tf_op jit(solution)/shard_map/reduce_scatter | solution.py:224
  2210.7 199.3 %reduce-scatter.49.cloned.1.call-done = f32[96,3072]{1,0:T(8,128)} async-done(((f32[1536,3072]{1,0:T(8,128)}), f32[96,3072]{1,0:T(8,128)}) %reduce-scatter.49.cloned.1.call-update) | async-done | bytes 1179664 | tf_op jit(solution)/shard_map/reduce_scatter | solution.py:223
  2410.0 79.5 %reduce-scatter.43.cloned.1.call-done = f32[768,96]{0,1:T(8,128)} async-done(((f32[768,1536]{0,1:T(8,128)}), f32[768,96]{0,1:T(8,128)}) %reduce-scatter.43.cloned.1.call-update) | async-done | bytes 294928 | tf_op jit(solution)/shard_map/reduce_scatter | solution.py:290
  2489.5 79.1 %reduce-scatter.41.cloned.1.call-done = f32[96,768]{1,0:T(8,128)} async-done(((f32[1536,768]{1,0:T(8,128)}), f32[96,768]{1,0:T(8,128)}) %reduce-scatter.41.cloned.1.call-update) | async-done | bytes 294928 | tf_op jit(solution)/shard_map/reduce_scatter | solution.py:289
  2568.5 79.6 %reduce-scatter.39.cloned.1.call-done = f32[96,768]{1,0:T(8,128)} async-done(((f32[1536,768]{1,0:T(8,128)}), f32[96,768]{1,0:T(8,128)}) %reduce-scatter.39.cloned.1.call-update) | async-done | bytes 294928 | tf_op jit(solution)/shard_map/reduce_scatter | solution.py:288
  2648.1 78.9 %reduce-scatter.37.cloned.1.call-done = f32[96,768]{1,0:T(8,128)} async-done(((f32[1536,768]{1,0:T(8,128)}), f32[96,768]{1,0:T(8,128)}) %reduce-scatter.37.cloned.1.call-update) | async-done | bytes 294928 | tf_op jit(solution)/shard_map/reduce_scatter | solution.py:287
  (334 shorter events, 536.1 us)
Async XLA Ops:
  36.7 120.8 %all-gather.23.cloned.1.call-start = ((), (), s32[]{:S(2)}) async-start(), calls=%async_computation.20 | async-start | bytes 2506752 | tf_op jit(solution)/shard_map/all_gather | solution.py:133
  37.4 163.4 %all-gather.21.cloned.1.call-start = ((), (), s32[]{:S(2)}) async-start(), calls=%async_computation.19 | async-start | bytes 2506752 | tf_op jit(solution)/shard_map/all_gather | solution.py:135
  38.0 206.1 %all-gather.27.cloned.1.call-start = ((), (), s32[]{:S(2)}) async-start(), calls=%async_computation.22 | async-start | bytes 2506752 | tf_op jit(solution)/shard_map/all_gather | solution.py:136
  38.6 270.3 %reduce-scatter.25.cloned.1.call-start = ((), (), s32[]{:S(2)}) async-start(), calls=%async_computation.23 | async-start | bytes 7077888 | tf_op jit(solution)/shard_map/reduce_scatter | solution.py:155
  250.0 103.8 %all-gather.29.cloned.1.call-start = ((), (), s32[]{:S(2)}) async-start(), calls=%async_computation.24 | async-start | bytes 2506752 | tf_op jit(solution)/shard_map/all_gather | solution.py:139
  250.7 146.7 %all-gather.35.cloned.1.call-start = ((), (), s32[]{:S(2)}) async-start(), calls=%async_computation.27 | async-start | bytes 2506752 | tf_op jit(solution)/shard_map/all_gather | solution.py:138
  251.5 189.7 %all-gather.33.cloned.1.call-start = ((), (), s32[]{:S(2)}) async-start(), calls=%async_computation.26 | async-start | bytes 2506752 | tf_op jit(solution)/shard_map/all_gather | solution.py:137
  252.2 225.9 %all-gather.31.cloned.1.call-start = ((), (), s32[]{:S(2)}) async-start(), calls=%async_computation.25 | async-start | bytes 3538944 | tf_op jit(solution)/shard_map/all_gather | solution.py:152
  313.0 209.9 %all-gather.37.cloned.1.call-start = ((), (), s32[]{:S(2)}) async-start(), calls=%async_computation.28 | async-start | bytes 2506752 | tf_op jit(solution)/shard_map/all_gather | solution.py:140
  313.8 274.3 %reduce-scatter.27.cloned.1.call-start = ((), (), s32[]{:S(2)}) async-start(), calls=%async_computation.29 | async-start | bytes 7077888 | tf_op jit(solution)/shard_map/reduce_scatter | solution.py:155
  529.2 142.7 %all-gather.41.cloned.1.call-start = ((), (), s32[]{:S(2)}) async-start(), calls=%async_computation.31 | async-start | bytes 10027008 | tf_op jit(solution)/shard_map/all_gather | solution.py:146
  529.9 178.2 %all-gather.39.cloned.1.call-start = ((), (), s32[]{:S(2)}) async-start(), calls=%async_computation.30 | async-start | bytes 3538944 | tf_op jit(solution)/shard_map/all_gather | solution.py:152
  593.1 198.6 %all-gather.43.cloned.1.call-start = ((), (), s32[]{:S(2)}) async-start(), calls=%async_computation.32 | async-start | bytes 10027008 | tf_op jit(solution)/shard_map/all_gather | solution.py:147
  593.7 279.7 %all-gather.45.cloned.1.call-start = ((), (), s32[]{:S(2)}) async-start(), calls=%async_computation.33 | async-start | bytes 10027008 | tf_op jit(solution)/shard_map/all_gather | solution.py:148
  594.3 351.8 %reduce-scatter.29.cloned.1.call-start = ((), (), s32[]{:S(2)}) async-start(), calls=%async_computation.34 | async-start | bytes 7077888 | tf_op jit(solution)/shard_map/reduce_scatter | solution.py:155
  949.7 139.7 %reduce-scatter.31.cloned.1.call-start = ((), (), s32[]{:S(2)}) async-start(), calls=%async_computation.36 | async-start | bytes 7077888 | tf_op jit(solution)/shard_map/reduce_scatter | solution.py:161
  1029.3 104.6 %all-gather.49.cloned.1.call-start = ((), (), s32[]{:S(2)}) async-start(), calls=%async_computation.37 | async-start | bytes 3538944 | tf_op jit(solution)/shard_map/all_gather | solution.py:158
  1097.6 114.1 %reduce-scatter.33.cloned.1.call-start = ((), (), s32[]{:S(2)}) async-start(), calls=%async_computation.38 | async-start | bytes 7077888 | tf_op jit(solution)/shard_map/reduce_scatter | solution.py:161
  1217.5 188.2 %reduce-scatter.35.cloned.1.call-start = ((), (), s32[]{:S(2)}) async-start(), calls=%async_computation.40 | async-start | bytes 7077888 | tf_op jit(solution)/shard_map/reduce_scatter | solution.py:161
  1345.6 216.8 %all-reduce.2.cloned.1.call-start = ((), (), s32[]{:S(2)}) async-start(), calls=%async_computation.41 | async-start | bytes 835584 | tf_op jit(solution)/shard_map/psum | solution.py:273
  1356.9 212.6 %reduce-scatter.59.cloned.1.call-start = ((), (), s32[]{:S(2)}) async-start(), calls=%async_computation.53 | async-start | bytes 835584
  1416.5 158.5 %reduce-scatter.47.cloned.1.call-start = ((), (), s32[]{:S(2)}) async-start(), calls=%async_computation.47 | async-start | bytes 5013504 | tf_op jit(solution)/shard_map/reduce_scatter | solution.py:294
  1422.8 231.1 %reduce-scatter.45.cloned.1.call-start = ((), (), s32[]{:S(2)}) async-start(), calls=%async_computation.46 | async-start | bytes 5013504 | tf_op jit(solution)/shard_map/reduce_scatter | solution.py:291
  1429.0 304.5 %reduce-scatter.57.cloned.1.call-start = ((), (), s32[]{:S(2)}) async-start(), calls=%async_computation.52 | async-start | bytes 5013504
  1438.0 374.6 %reduce-scatter.55.cloned.1.call-start = ((), (), s32[]{:S(2)}) async-start(), calls=%async_computation.51 | async-start | bytes 5013504
  1447.3 564.2 %reduce-scatter.53.cloned.1.call-start = ((), (), s32[]{:S(2)}) async-start(), calls=%async_computation.50 | async-start | bytes 20054016 | tf_op jit(solution)/shard_map/reduce_scatter | solution.py:225
  1461.8 748.9 %reduce-scatter.51.cloned.1.call-start = ((), (), s32[]{:S(2)}) async-start(), calls=%async_computation.49 | async-start | bytes 20054016 | tf_op jit(solution)/shard_map/reduce_scatter | solution.py:224
  1475.7 934.3 %reduce-scatter.49.cloned.1.call-start = ((), (), s32[]{:S(2)}) async-start(), calls=%async_computation.48 | async-start | bytes 20054016 | tf_op jit(solution)/shard_map/reduce_scatter | solution.py:223
  1489.7 999.8 %reduce-scatter.43.cloned.1.call-start = ((), (), s32[]{:S(2)}) async-start(), calls=%async_computation.45 | async-start | bytes 5013504 | tf_op jit(solution)/shard_map/reduce_scatter | solution.py:290
  1497.0 1071.5 %reduce-scatter.41.cloned.1.call-start = ((), (), s32[]{:S(2)}) async-start(), calls=%async_computation.44 | async-start | bytes 5013504 | tf_op jit(solution)/shard_map/reduce_scatter | solution.py:289
  1504.2 1143.9 %reduce-scatter.39.cloned.1.call-start = ((), (), s32[]{:S(2)}) async-start(), calls=%async_computation.43 | async-start | bytes 5013504 | tf_op jit(solution)/shard_map/reduce_scatter | solution.py:288
  1511.5 1215.5 %reduce-scatter.37.cloned.1.call-start = ((), (), s32[]{:S(2)}) async-start(), calls=%async_computation.42 | async-start | bytes 5013504 | tf_op jit(solution)/shard_map/reduce_scatter | solution.py:287
  (80 other events, 2854.4 us)
Sparse Core Ops, SparseCore 0:
  71.7 42.3 all-gather.24
  116.4 41.0 all-gather.22
  159.7 41.0 all-gather.20
  202.9 41.0 all-gather.26
  250.1 58.7 reduce-scatter.24
  311.4 42.3 all-gather.28
  356.3 41.0 all-gather.34
  400.0 41.0 all-gather.32
  480.6 42.3 all-gather.36
  529.3 58.7 reduce-scatter.26
  590.4 81.4 all-gather.40
  710.2 81.4 all-gather.42
  793.8 79.5 all-gather.44
  886.5 59.5 reduce-scatter.28
  949.8 35.8 all-gather.46
  1029.4 59.9 reduce-scatter.30
  1097.7 36.0 all-gather.48
  1151.6 59.9 reduce-scatter.32
  1217.6 36.0 all-gather.50
  1345.7 59.9 reduce-scatter.34
  1438.3 56.7 reduce-scatter.58
  1499.8 75.1 reduce-scatter.46
  1579.3 74.5 reduce-scatter.44
  1658.8 74.6 reduce-scatter.56
  1737.9 74.6 reduce-scatter.54
  1817.7 193.8 reduce-scatter.52
  2016.8 193.8 reduce-scatter.50
  2215.9 194.0 reduce-scatter.48
  2414.8 74.6 reduce-scatter.42
  2493.9 74.5 reduce-scatter.40
  2573.5 74.5 reduce-scatter.38
  2652.4 74.5 reduce-scatter.36
  (4 shorter events, 128.5 us)
where the time goes:
time: 2740 us
  waiting for transfers between devices  2170 us (79%)
  matrix products  319 us (12%)
  blocking collectives  111 us (4%)
  other arithmetic  78.4 us (3%)
  local copies, waits for them, and re-layouts  35.4 us (1%)
    reduce_scatter x1, waiting for transfers between devices, body(): lax.psum_scatter(grad_gate_w, 'dp', scatter_dimension=0, tiled=True)  199 us
    reduce_scatter x1, waiting for transfers between devices, body(): lax.psum_scatter(grad_up_w, 'dp', scatter_dimension=0, tiled=True)  199 us
    reduce_scatter x1, waiting for transfers between devices, body(): lax.psum_scatter(grad_down, 'dp', scatter_dimension=1, tiled=True)  199 us
    reduce_scatter x3, waiting for transfers between devices, scatter_grads(): return lax.psum_scatter(values, 'tensor', scatter_dimension=0, tiled=True)  169 us
    unnamed x39, waiting for transfers between devices  166 us
    reduce_scatter x3, waiting for transfers between devices, scatter_rows(): return lax.psum_scatter(values, 'tensor', scatter_dimension=0, tiled=True)  133 us
    all_gather x3, waiting for transfers between devices, gather_grads(): return lax.all_gather(values, 'tensor', axis=0, tiled=True)  107 us
    all_gather x3, waiting for transfers between devices, gather_rows(): return lax.all_gather(values, 'tensor', axis=0, tiled=True)  103 us
  transfers between devices with their start and end apart: 36, of which 34 were waited for; matrix products, arithmetic and copies ran while one was open for 8% of the time, Pallas kernels for 0%

commit v1 on v0

--- a/solution.py
+++ b/solution.py
@@ -203,7 +203,9 @@
     block_out = hidden_two + scatter_rows(matmul(hidden_ff, weight_down))
     error_diff = block_out - teacher[0].astype(jnp.float32)
     local_error = jnp.sum(mask_float[:, None] * error_diff * error_diff)
-    valid_count, error_total = lax.psum((jnp.sum(mask_float), local_error), ("dp", "tensor"))
+    valid_count, error_total = lax.psum(
+        lax.psum((jnp.sum(mask_float), local_error), "tensor"), "dp"
+    )
     mean_loss = error_total / (width * valid_count)
     grad_out = 2.0 * token_total / valid_count * mask_float[:, None] * error_diff
     weight_gate, weight_up, weight_down = fetch_mlp()

time: 2740 us -> 2740 us (level)
    psum x2 -> x4, blocking collectives: 81.2 us -> 73.2 us  [the longest x2 62.1 us: body(): lax.psum(lax.psum((jnp.sum(mask_float), local_error), 'tensor'), 'dp')]
where the time goes in v1:
time: 2740 us; the launch traced here: 2730 us
  waiting for transfers between devices  2180 us (80%)
  matrix products  319 us (12%)
  blocking collectives  103 us (4%)
  other arithmetic  78.3 us (3%)
  local copies, waits for them, and re-layouts  35.4 us (1%)
    reduce_scatter x1, waiting for transfers between devices, body(): lax.psum_scatter(grad_gate_w, 'dp', scatter_dimension=0, tiled=True)  199 us
    reduce_scatter x1, waiting for transfers between devices, body(): lax.psum_scatter(grad_down, 'dp', scatter_dimension=1, tiled=True)  199 us
    reduce_scatter x1, waiting for transfers between devices, body(): lax.psum_scatter(grad_up_w, 'dp', scatter_dimension=0, tiled=True)  199 us
    reduce_scatter x3, waiting for transfers between devices, scatter_grads(): return lax.psum_scatter(values, 'tensor', scatter_dimension=0, tiled=True)  169 us
    unnamed x39, waiting for transfers between devices  166 us
    reduce_scatter x3, waiting for transfers between devices, scatter_rows(): return lax.psum_scatter(values, 'tensor', scatter_dimension=0, tiled=True)  135 us
    all_gather x3, waiting for transfers between devices, gather_grads(): return lax.all_gather(values, 'tensor', axis=0, tiled=True)  108 us
    all_gather x3, waiting for transfers between devices, gather_rows(): return lax.all_gather(values, 'tensor', axis=0, tiled=True)  103 us
  transfers between devices with their start and end apart: 36, of which 34 were waited for; matrix products, arithmetic and copies ran while one was open for 8% of the time, Pallas kernels for 0%

profile of v1, /device:TPU:0, one launch (start us, length us, event | category | flops | bytes accessed | tf_op | source)
XLA Modules:
  0.0 2733.9 jit_solution(10189647838008856258)
XLA Ops:
  39.1 30.3 %all-gather.19.cloned.1.call-done = bf16[768,1536]{1,0:T(8,128)(2,1)} async-done(((bf16[384,1536]{1,0:T(8,128)(2,1)}), bf16[768,1536]{1,0:T(8,128)(2,1)}) %all-gather.19.cloned.1.call-update) | async-done | bytes 2359312 | tf_op jit(solution)/shard_map/all_gather | solution.py:152
  69.5 44.6 %all-gather.25.cloned.1.call-done = bf16[1536,768]{1,0:T(8,128)(2,1)} async-done(((bf16[96,768]{1,0:T(8,128)(2,1)}), bf16[1536,768]{1,0:T(8,128)(2,1)}) %all-gather.25.cloned.1.call-update) | async-done | bytes 2359312 | tf_op jit(solution)/shard_map/all_gather | solution.py:134
  118.6 38.9 %all-gather.23.cloned.1.call-done = bf16[1536,768]{1,0:T(8,128)(2,1)} async-done(((bf16[96,768]{1,0:T(8,128)(2,1)}), bf16[1536,768]{1,0:T(8,128)(2,1)}) %all-gather.23.cloned.1.call-update) | async-done | bytes 2359312 | tf_op jit(solution)/shard_map/all_gather | solution.py:133
  252.2 56.6 %reduce-scatter.25.cloned.1.call-done = f32[384,1536]{1,0:T(8,128)} async-done(((f32[768,1536]{1,0:T(8,128)}), f32[384,1536]{1,0:T(8,128)}) %reduce-scatter.25.cloned.1.call-update) | async-done | bytes 2359312 | tf_op jit(solution)/shard_map/reduce_scatter | solution.py:155
  314.0 39.8 %all-gather.29.cloned.1.call-done = bf16[1536,768]{1,0:T(8,128)(2,1)} async-done(((bf16[96,768]{1,0:T(8,128)(2,1)}), bf16[1536,768]{1,0:T(8,128)(2,1)}) %all-gather.29.cloned.1.call-update) | async-done | bytes 2359312 | tf_op jit(solution)/shard_map/all_gather | solution.py:139
  356.9 40.6 %all-gather.35.cloned.1.call-done = bf16[1536,768]{1,0:T(8,128)(2,1)} async-done(((bf16[96,768]{1,0:T(8,128)(2,1)}), bf16[1536,768]{1,0:T(8,128)(2,1)}) %all-gather.35.cloned.1.call-update) | async-done | bytes 2359312 | tf_op jit(solution)/shard_map/all_gather | solution.py:138
  399.8 41.3 %all-gather.33.cloned.1.call-done = bf16[1536,768]{1,0:T(8,128)(2,1)} async-done(((bf16[96,768]{1,0:T(8,128)(2,1)}), bf16[1536,768]{1,0:T(8,128)(2,1)}) %all-gather.33.cloned.1.call-update) | async-done | bytes 2359312 | tf_op jit(solution)/shard_map/all_gather | solution.py:137
  441.1 36.9 %all-gather.31.cloned.1.call-done = bf16[768,1536]{1,0:T(8,128)(2,1)} async-done(((bf16[384,1536]{1,0:T(8,128)(2,1)}), bf16[768,1536]{1,0:T(8,128)(2,1)}) %all-gather.31.cloned.1.call-update) | async-done | bytes 2359312 | tf_op jit(solution)/shard_map/all_gather | solution.py:152
  488.3 34.7 %all-gather.37.cloned.1.call-done = bf16[768,1536]{0,1:T(8,128)(2,1)} async-done(((bf16[768,96]{0,1:T(8,128)(2,1)}), bf16[768,1536]{0,1:T(8,128)(2,1)}) %all-gather.37.cloned.1.call-update) | async-done | bytes 2359312 | tf_op jit(solution)/shard_map/all_gather | solution.py:140
  530.0 58.1 %reduce-scatter.27.cloned.1.call-done = f32[384,1536]{1,0:T(8,128)} async-done(((f32[768,1536]{1,0:T(8,128)}), f32[384,1536]{1,0:T(8,128)}) %reduce-scatter.27.cloned.1.call-update) | async-done | bytes 2359312 | tf_op jit(solution)/shard_map/reduce_scatter | solution.py:155
  594.5 77.3 %all-gather.41.cloned.1.call-done = bf16[1536,3072]{1,0:T(8,128)(2,1)} async-done(((bf16[96,3072]{1,0:T(8,128)(2,1)}), bf16[1536,3072]{1,0:T(8,128)(2,1)}) %all-gather.41.cloned.1.call-update) | async-done | bytes 9437200 | tf_op jit(solution)/shard_map/all_gather | solution.py:146
  671.9 36.2 %all-gather.39.cloned.1.call-done = bf16[768,1536]{1,0:T(8,128)(2,1)} async-done(((bf16[384,1536]{1,0:T(8,128)(2,1)}), bf16[768,1536]{1,0:T(8,128)(2,1)}) %all-gather.39.cloned.1.call-update) | async-done | bytes 2359312 | tf_op jit(solution)/shard_map/all_gather | solution.py:152
  722.1 69.6 %all-gather.43.cloned.1.call-done = bf16[1536,3072]{1,0:T(8,128)(2,1)} async-done(((bf16[96,3072]{1,0:T(8,128)(2,1)}), bf16[1536,3072]{1,0:T(8,128)(2,1)}) %all-gather.43.cloned.1.call-update) | async-done | bytes 9437200 | tf_op jit(solution)/shard_map/all_gather | solution.py:147
  808.0 65.4 %all-gather.45.cloned.1.call-done = bf16[3072,1536]{0,1:T(8,128)(2,1)} async-done(((bf16[3072,96]{0,1:T(8,128)(2,1)}), bf16[3072,1536]{0,1:T(8,128)(2,1)}) %all-gather.45.cloned.1.call-update) | async-done | bytes 9437200 | tf_op jit(solution)/shard_map/all_gather | solution.py:148
  893.2 30.3 %psum.45 = f32[]{:T(128)} all-reduce(f32[]{:T(128)} %psum.44), channel_id=1, replica_groups=mesh['dp'=16,'tensor'=2] {'dp'}, use_global_device_ids=true, to_apply=%region_18.0 | all-reduce | flops 1 | bytes 8 | tf_op jit(solution)/shard_map/psum | solution.py:206
  948.8 35.7 %all-gather.47.cloned.1.call-done = bf16[768,1536]{1,0:T(8,128)(2,1)} async-done(((bf16[384,1536]{1,0:T(8,128)(2,1)}), bf16[768,1536]{1,0:T(8,128)(2,1)}) %all-gather.47.cloned.1.call-update) | async-done | bytes 2359312 | tf_op jit(solution)/shard_map/all_gather | solution.py:158
  1028.1 60.1 %reduce-scatter.31.cloned.1.call-done = f32[384,1536]{1,0:T(8,128)} async-done(((f32[768,1536]{1,0:T(8,128)}), f32[384,1536]{1,0:T(8,128)}) %reduce-scatter.31.cloned.1.call-update) | async-done | bytes 2359312 | tf_op jit(solution)/shard_map/reduce_scatter | solution.py:161
  1096.7 36.0 %all-gather.49.cloned.1.call-done = bf16[768,1536]{1,0:T(8,128)(2,1)} async-done(((bf16[384,1536]{1,0:T(8,128)(2,1)}), bf16[768,1536]{1,0:T(8,128)(2,1)}) %all-gather.49.cloned.1.call-update) | async-done | bytes 2359312 | tf_op jit(solution)/shard_map/all_gather | solution.py:158
  1150.3 60.1 %reduce-scatter.33.cloned.1.call-done = f32[384,1536]{1,0:T(8,128)} async-done(((f32[768,1536]{1,0:T(8,128)}), f32[384,1536]{1,0:T(8,128)}) %reduce-scatter.33.cloned.1.call-update) | async-done | bytes 2359312 | tf_op jit(solution)/shard_map/reduce_scatter | solution.py:161
  1216.5 35.9 %all-gather.51.cloned.1.call-done = bf16[768,1536]{1,0:T(8,128)(2,1)} async-done(((bf16[384,1536]{1,0:T(8,128)(2,1)}), bf16[768,1536]{1,0:T(8,128)(2,1)}) %all-gather.51.cloned.1.call-update) | async-done | bytes 2359312 | tf_op jit(solution)/shard_map/all_gather | solution.py:158
  1355.7 48.8 %reduce-scatter.35.cloned.1.call-done = f32[384,1536]{1,0:T(8,128)} async-done(((f32[768,1536]{1,0:T(8,128)}), f32[384,1536]{1,0:T(8,128)}) %reduce-scatter.35.cloned.1.call-update) | async-done | bytes 2359312 | tf_op jit(solution)/shard_map/reduce_scatter | solution.py:161
  1523.7 31.8 %psum.43 = f32[]{:T(128)} all-reduce(f32[]{:T(128)} %psum.42), channel_id=1, replica_groups=mesh['dp'=16,'tensor'=2] {'dp'}, use_global_device_ids=true, to_apply=%region_15.0 | all-reduce | flops 1 | bytes 8 | tf_op jit(solution)/shard_map/psum | solution.py:206
  1573.7 78.9 %reduce-scatter.45.cloned.1.call-done = f32[96,768]{1,0:T(8,128)} async-done(((f32[1536,768]{1,0:T(8,128)}), f32[96,768]{1,0:T(8,128)}) %reduce-scatter.45.cloned.1.call-update) | async-done | bytes 294928 | tf_op jit(solution)/shard_map/reduce_scatter | solution.py:293
  1652.6 79.6 %reduce-scatter.57.cloned.1.call-done = f32[96,768]{1,0:T(8,128)} async-done(((f32[1536,768]{1,0:T(8,128)}), f32[96,768]{1,0:T(8,128)}) %reduce-scatter.57.cloned.1.call-update) | async-done | bytes 294928
  1732.2 79.1 %reduce-scatter.55.cloned.1.call-done = f32[96,768]{1,0:T(8,128)} async-done(((f32[1536,768]{1,0:T(8,128)}), f32[96,768]{1,0:T(8,128)}) %reduce-scatter.55.cloned.1.call-update) | async-done | bytes 294928
  1811.2 199.1 %reduce-scatter.53.cloned.1.call-done = f32[3072,96]{0,1:T(8,128)} async-done(((f32[3072,1536]{0,1:T(8,128)}), f32[3072,96]{0,1:T(8,128)}) %reduce-scatter.53.cloned.1.call-update) | async-done | bytes 1179664 | tf_op jit(solution)/shard_map/reduce_scatter | solution.py:227
  2010.4 199.1 %reduce-scatter.51.cloned.1.call-done = f32[96,3072]{1,0:T(8,128)} async-done(((f32[1536,3072]{1,0:T(8,128)}), f32[96,3072]{1,0:T(8,128)}) %reduce-scatter.51.cloned.1.call-update) | async-done | bytes 1179664 | tf_op jit(solution)/shard_map/reduce_scatter | solution.py:226
  2209.5 199.3 %reduce-scatter.49.cloned.1.call-done = f32[96,3072]{1,0:T(8,128)} async-done(((f32[1536,3072]{1,0:T(8,128)}), f32[96,3072]{1,0:T(8,128)}) %reduce-scatter.49.cloned.1.call-update) | async-done | bytes 1179664 | tf_op jit(solution)/shard_map/reduce_scatter | solution.py:225
  2408.8 79.5 %reduce-scatter.43.cloned.1.call-done = f32[768,96]{0,1:T(8,128)} async-done(((f32[768,1536]{0,1:T(8,128)}), f32[768,96]{0,1:T(8,128)}) %reduce-scatter.43.cloned.1.call-update) | async-done | bytes 294928 | tf_op jit(solution)/shard_map/reduce_scatter | solution.py:292
  2488.3 79.1 %reduce-scatter.41.cloned.1.call-done = f32[96,768]{1,0:T(8,128)} async-done(((f32[1536,768]{1,0:T(8,128)}), f32[96,768]{1,0:T(8,128)}) %reduce-scatter.41.cloned.1.call-update) | async-done | bytes 294928 | tf_op jit(solution)/shard_map/reduce_scatter | solution.py:291
  2567.3 79.6 %reduce-scatter.39.cloned.1.call-done = f32[96,768]{1,0:T(8,128)} async-done(((f32[1536,768]{1,0:T(8,128)}), f32[96,768]{1,0:T(8,128)}) %reduce-scatter.39.cloned.1.call-update) | async-done | bytes 294928 | tf_op jit(solution)/shard_map/reduce_scatter | solution.py:290
  2646.9 78.9 %reduce-scatter.37.cloned.1.call-done = f32[96,768]{1,0:T(8,128)} async-done(((f32[1536,768]{1,0:T(8,128)}), f32[96,768]{1,0:T(8,128)}) %reduce-scatter.37.cloned.1.call-update) | async-done | bytes 294928 | tf_op jit(solution)/shard_map/reduce_scatter | solution.py:289
  (336 shorter events, 553.7 us)
Async XLA Ops:
  36.7 120.8 %all-gather.23.cloned.1.call-start = ((), (), s32[]{:S(2)}) async-start(), calls=%async_computation.20 | async-start | bytes 2506752 | tf_op jit(solution)/shard_map/all_gather | solution.py:133
  37.4 163.4 %all-gather.21.cloned.1.call-start = ((), (), s32[]{:S(2)}) async-start(), calls=%async_computation.19 | async-start | bytes 2506752 | tf_op jit(solution)/shard_map/all_gather | solution.py:135
  38.0 206.1 %all-gather.27.cloned.1.call-start = ((), (), s32[]{:S(2)}) async-start(), calls=%async_computation.22 | async-start | bytes 2506752 | tf_op jit(solution)/shard_map/all_gather | solution.py:136
  38.6 270.3 %reduce-scatter.25.cloned.1.call-start = ((), (), s32[]{:S(2)}) async-start(), calls=%async_computation.23 | async-start | bytes 7077888 | tf_op jit(solution)/shard_map/reduce_scatter | solution.py:155
  249.9 103.8 %all-gather.29.cloned.1.call-start = ((), (), s32[]{:S(2)}) async-start(), calls=%async_computation.24 | async-start | bytes 2506752 | tf_op jit(solution)/shard_map/all_gather | solution.py:139
  250.7 146.8 %all-gather.35.cloned.1.call-start = ((), (), s32[]{:S(2)}) async-start(), calls=%async_computation.27 | async-start | bytes 2506752 | tf_op jit(solution)/shard_map/all_gather | solution.py:138
  251.4 189.7 %all-gather.33.cloned.1.call-start = ((), (), s32[]{:S(2)}) async-start(), calls=%async_computation.26 | async-start | bytes 2506752 | tf_op jit(solution)/shard_map/all_gather | solution.py:137
  252.2 225.9 %all-gather.31.cloned.1.call-start = ((), (), s32[]{:S(2)}) async-start(), calls=%async_computation.25 | async-start | bytes 3538944 | tf_op jit(solution)/shard_map/all_gather | solution.py:152
  313.0 209.9 %all-gather.37.cloned.1.call-start = ((), (), s32[]{:S(2)}) async-start(), calls=%async_computation.28 | async-start | bytes 2506752 | tf_op jit(solution)/shard_map/all_gather | solution.py:140
  313.7 274.3 %reduce-scatter.27.cloned.1.call-start = ((), (), s32[]{:S(2)}) async-start(), calls=%async_computation.29 | async-start | bytes 7077888 | tf_op jit(solution)/shard_map/reduce_scatter | solution.py:155
  529.2 142.7 %all-gather.41.cloned.1.call-start = ((), (), s32[]{:S(2)}) async-start(), calls=%async_computation.31 | async-start | bytes 10027008 | tf_op jit(solution)/shard_map/all_gather | solution.py:146
  529.9 178.2 %all-gather.39.cloned.1.call-start = ((), (), s32[]{:S(2)}) async-start(), calls=%async_computation.30 | async-start | bytes 3538944 | tf_op jit(solution)/shard_map/all_gather | solution.py:152
  593.1 198.6 %all-gather.43.cloned.1.call-start = ((), (), s32[]{:S(2)}) async-start(), calls=%async_computation.32 | async-start | bytes 10027008 | tf_op jit(solution)/shard_map/all_gather | solution.py:147
  593.7 279.7 %all-gather.45.cloned.1.call-start = ((), (), s32[]{:S(2)}) async-start(), calls=%async_computation.33 | async-start | bytes 10027008 | tf_op jit(solution)/shard_map/all_gather | solution.py:148
  594.3 350.5 %reduce-scatter.29.cloned.1.call-start = ((), (), s32[]{:S(2)}) async-start(), calls=%async_computation.34 | async-start | bytes 7077888 | tf_op jit(solution)/shard_map/reduce_scatter | solution.py:155
  948.3 139.9 %reduce-scatter.31.cloned.1.call-start = ((), (), s32[]{:S(2)}) async-start(), calls=%async_computation.36 | async-start | bytes 7077888 | tf_op jit(solution)/shard_map/reduce_scatter | solution.py:161
  1028.1 104.6 %all-gather.49.cloned.1.call-start = ((), (), s32[]{:S(2)}) async-start(), calls=%async_computation.37 | async-start | bytes 3538944 | tf_op jit(solution)/shard_map/all_gather | solution.py:158
  1096.4 114.0 %reduce-scatter.33.cloned.1.call-start = ((), (), s32[]{:S(2)}) async-start(), calls=%async_computation.38 | async-start | bytes 7077888 | tf_op jit(solution)/shard_map/reduce_scatter | solution.py:161
  1216.2 188.2 %reduce-scatter.35.cloned.1.call-start = ((), (), s32[]{:S(2)}) async-start(), calls=%async_computation.40 | async-start | bytes 7077888 | tf_op jit(solution)/shard_map/reduce_scatter | solution.py:161
  1344.3 211.9 %all-reduce.2.cloned.1.call-start = ((), (), s32[]{:S(2)}) async-start(), calls=%async_computation.41 | async-start | bytes 835584 | tf_op jit(solution)/shard_map/psum | solution.py:275
  1355.6 207.7 %reduce-scatter.59.cloned.1.call-start = ((), (), s32[]{:S(2)}) async-start(), calls=%async_computation.53 | async-start | bytes 835584
  1415.2 158.5 %reduce-scatter.47.cloned.1.call-start = ((), (), s32[]{:S(2)}) async-start(), calls=%async_computation.47 | async-start | bytes 5013504 | tf_op jit(solution)/shard_map/reduce_scatter | solution.py:296
  1421.5 231.1 %reduce-scatter.45.cloned.1.call-start = ((), (), s32[]{:S(2)}) async-start(), calls=%async_computation.46 | async-start | bytes 5013504 | tf_op jit(solution)/shard_map/reduce_scatter | solution.py:293
  1427.7 304.4 %reduce-scatter.57.cloned.1.call-start = ((), (), s32[]{:S(2)}) async-start(), calls=%async_computation.52 | async-start | bytes 5013504
  1436.8 374.5 %reduce-scatter.55.cloned.1.call-start = ((), (), s32[]{:S(2)}) async-start(), calls=%async_computation.51 | async-start | bytes 5013504
  1446.0 564.3 %reduce-scatter.53.cloned.1.call-start = ((), (), s32[]{:S(2)}) async-start(), calls=%async_computation.50 | async-start | bytes 20054016 | tf_op jit(solution)/shard_map/reduce_scatter | solution.py:227
  1460.5 749.0 %reduce-scatter.51.cloned.1.call-start = ((), (), s32[]{:S(2)}) async-start(), calls=%async_computation.49 | async-start | bytes 20054016 | tf_op jit(solution)/shard_map/reduce_scatter | solution.py:226
  1474.5 934.3 %reduce-scatter.49.cloned.1.call-start = ((), (), s32[]{:S(2)}) async-start(), calls=%async_computation.48 | async-start | bytes 20054016 | tf_op jit(solution)/shard_map/reduce_scatter | solution.py:225
  1488.4 999.9 %reduce-scatter.43.cloned.1.call-start = ((), (), s32[]{:S(2)}) async-start(), calls=%async_computation.45 | async-start | bytes 5013504 | tf_op jit(solution)/shard_map/reduce_scatter | solution.py:292
  1495.7 1071.6 %reduce-scatter.41.cloned.1.call-start = ((), (), s32[]{:S(2)}) async-start(), calls=%async_computation.44 | async-start | bytes 5013504 | tf_op jit(solution)/shard_map/reduce_scatter | solution.py:291
  1502.9 1144.0 %reduce-scatter.39.cloned.1.call-start = ((), (), s32[]{:S(2)}) async-start(), calls=%async_computation.43 | async-start | bytes 5013504 | tf_op jit(solution)/shard_map/reduce_scatter | solution.py:290
  1510.3 1215.5 %reduce-scatter.37.cloned.1.call-start = ((), (), s32[]{:S(2)}) async-start(), calls=%async_computation.42 | async-start | bytes 5013504 | tf_op jit(solution)/shard_map/reduce_scatter | solution.py:289
  (80 other events, 2851.8 us)
Sparse Core Ops, SparseCore 0:
  71.7 42.3 all-gather.24
  116.4 41.0 all-gather.22
  159.7 41.0 all-gather.20
  202.9 41.0 all-gather.26
  250.0 58.7 reduce-scatter.24
  311.4 42.3 all-gather.28
  356.3 41.0 all-gather.34
  400.0 41.0 all-gather.32
  480.6 42.3 all-gather.36
  529.3 58.7 reduce-scatter.26
  590.4 81.4 all-gather.40
  710.2 81.4 all-gather.42
  793.8 79.5 all-gather.44
  886.5 58.1 reduce-scatter.28
  948.5 35.9 all-gather.46
  1028.2 59.9 reduce-scatter.30
  1096.5 36.0 all-gather.48
  1150.4 59.9 reduce-scatter.32
  1216.3 36.0 all-gather.50
  1344.4 59.9 reduce-scatter.34
  1437.0 56.6 reduce-scatter.58
  1498.5 75.1 reduce-scatter.46
  1578.0 74.5 reduce-scatter.44
  1657.5 74.5 reduce-scatter.56
  1736.6 74.5 reduce-scatter.54
  1816.3 193.9 reduce-scatter.52
  2015.6 193.8 reduce-scatter.50
  2214.7 194.0 reduce-scatter.48
  2413.6 74.6 reduce-scatter.42
  2492.7 74.5 reduce-scatter.40
  2572.3 74.5 reduce-scatter.38
  2651.2 74.5 reduce-scatter.36
  (4 shorter events, 128.5 us)
